TPU v7x, 32 devices: a whole 2x2x4 slice. The times are simulated.
32 devices in a mesh: fsdp: 4 (over z), context: 4 (over y, x), tensor: 2 (over core).
Axes of the slice: x: 2, y: 2, z: 4, core: 2. Of those that a mesh axis runs over, the one named last changes fastest.
Arguments:
- tokens: float32 [12, 1408, 1024], P('fsdp', 'context'), may hold values from -6 to 6
- cotangent: float32 [12, 1408, 1024], P('fsdp', 'context'), may hold values from -6 to 6
- gains: float32 [4, 1024], replicated, may hold values from 0.5 to 1.5
- w_qkv: bfloat16 [1024, 3, 1024], P('fsdp', None, 'tensor'), may hold values from -0.1875 to 0.1875
- w_out: bfloat16 [1024, 1024], P('tensor', 'fsdp'), may hold values from -4 to 4
- w_up: bfloat16 [1024, 4096], P('fsdp', 'tensor'), may hold values from -0.1875 to 0.1875
- w_down: bfloat16 [4096, 1024], P('tensor', 'fsdp'), may hold values from -0.09375 to 0.09375
- key_mask: int32 [12, 1408], P('fsdp', 'context'), may hold values from 0 to 1, as said below
- owner: int32 [12], replicated, may hold values from 0 to 11, each once
- stat_left: float32 [12, 2, 512, 1024], P('context', 'tensor', 'fsdp'), may hold values from -120 to 640
- stat_right: float32 [12, 2, 512, 1024], P('context', 'tensor', 'fsdp'), may hold values from -120 to 640
- root_left: float32 [12, 2, 512, 1024], P('context', 'tensor', 'fsdp'), may hold values from -3 to 24
- root_right: float32 [12, 1024, 1024], P('context'), may hold values from -0.3 to 1.6
- master: float32 [12, 2, 512, 1024], P('context', 'tensor', 'fsdp'), may hold values from -6 to 6
- gain_state: float32 [4, 1024], P(None, ('fsdp', 'context')), may hold values from 0.5 to 4
Outputs:
- output: float32 [12, 1408, 1024], P('fsdp', 'context')
- grad_tokens: float32 [12, 1408, 1024], P('fsdp', 'context')
- grad_blocks: float32 [12, 2, 512, 1024], P('context', 'tensor', 'fsdp')
- stat_left_new: float32 [12, 2, 512, 1024], P('context', 'tensor', 'fsdp')
- stat_right_new: float32 [12, 2, 512, 1024], P('context', 'tensor', 'fsdp')
- weight_new: float32 [12, 2, 512, 1024], P('context', 'tensor', 'fsdp')
- gain_grad: float32 [4, 1024], P(None, ('fsdp', 'context'))
- gain_state_new: float32 [4, 1024], P(None, ('fsdp', 'context'))
- gain_new: float32 [4, 1024], P(None, ('fsdp', 'context'))
Inputs may be any that keep to these rules, and one draw needn't show every extreme that they name: `key_mask`: each image's real tokens are its first p * p + 1 positions, for a whole p from 28 to 37; some image has p = 37.
All inputs are finite; a program needn't handle non-finite values.
Results may differ from a plain program's by a relative error of at most 0.012.
Values may be sent and summed in bfloat16 or wider, within the bound.
A program may use at most 256 MiB of HBM per device.

v0:
```python
import jax
import jax.numpy as jnp
from jax import lax
from jax.sharding import PartitionSpec as P

D = 1024
HD = 64
SEQ = 1408
NBLK = 12


def norm_fwd(field_in, gain_vec):
    centred = field_in - jnp.mean(field_in, axis=-1, keepdims=True)
    inv_std = lax.rsqrt(jnp.mean(centred * centred, axis=-1, keepdims=True) + 1e-06)
    normed = centred * inv_std
    return (normed, inv_std, normed * gain_vec)


def norm_back(grad_out, gain_vec, normed, inv_std):
    scaled = grad_out * gain_vec
    inner_sum = (
        scaled
        - jnp.mean(scaled, axis=-1, keepdims=True)
        - normed * jnp.mean(scaled * normed, axis=-1, keepdims=True)
    )
    return (inner_sum * inv_std, jnp.sum(grad_out * normed, axis=(0, 1)))


def gelu_parts(field_in):
    normal_cdf = 0.5 * (1.0 + lax.erf(field_in * 0.7071067811865476))
    normal_pdf = jnp.exp(-0.5 * field_in * field_in) * 0.3989422804014327
    return (field_in * normal_cdf, normal_cdf + field_in * normal_pdf)


def split_heads(field_in):
    shaped = field_in.reshape(field_in.shape[0], field_in.shape[1], field_in.shape[2] // HD, HD)
    return jnp.moveaxis(shaped, 2, 0)


def join_heads(field_in):
    moved_axes = jnp.moveaxis(field_in, 0, 2)
    return moved_axes.reshape(moved_axes.shape[0], moved_axes.shape[1], -1)


def per_device(
    tokens,
    cotangent,
    gains,
    w_qkv,
    w_out,
    w_up,
    w_down,
    key_mask,
    owner,
    stat_left,
    stat_right,
    root_left,
    root_right,
    master,
    gain_state,
):
    images = tokens.shape[0]
    local_len = tokens.shape[1]
    tok_rows = images * local_len
    score_scale = HD ** (-0.5)
    qkv_full, out_full, up_full, down_full = (
        lax.all_gather(w_qkv, "fsdp", axis=0, tiled=True),
        lax.all_gather(w_out, "fsdp", axis=1, tiled=True),
        lax.all_gather(w_up, "fsdp", axis=0, tiled=True),
        lax.all_gather(w_down, "fsdp", axis=1, tiled=True),
    )
    half_width = qkv_full.shape[2]
    hidden = up_full.shape[1]
    up_blocks = hidden // half_width
    normed1, inv_std1, pre_norm1 = norm_fwd(tokens, gains[0])
    normed1_low = pre_norm1.astype(jnp.bfloat16)
    qkv = jnp.einsum(
        "isd,djh->isjh", normed1_low, qkv_full, preferred_element_type=jnp.float32
    ).astype(jnp.bfloat16)
    kv_local = qkv[:, :, 1:]
    key_flag = key_mask.astype(jnp.bfloat16)
    keys_vals, key_live = (
        lax.all_gather(kv_local, "context", axis=1, tiled=True),
        lax.all_gather(key_flag, "context", axis=1, tiled=True),
    )

    def head_forward(operands):
        queries, key_rows, value_rows = operands
        scores = (
            jnp.einsum("iqd,ikd->iqk", queries, key_rows, preferred_element_type=jnp.float32)
            * score_scale
        )
        scores = jnp.where(key_live[:, None, :] > 0, scores, -1e30)
        peak_val = jnp.max(scores, axis=-1, keepdims=True)
        expo_val = jnp.exp(scores - peak_val)
        totals = jnp.sum(expo_val, axis=-1, keepdims=True)
        prob_low = (expo_val / totals).astype(jnp.bfloat16)
        mixed = jnp.einsum("iqk,ikd->iqd", prob_low, value_rows, preferred_element_type=jnp.float32)
        return (mixed, peak_val + jnp.log(totals))

    query_heads = split_heads(qkv[:, :, 0])
    head_out, log_total = lax.map(
        head_forward,
        (query_heads, split_heads(keys_vals[:, :, 0]), split_heads(keys_vals[:, :, 1])),
    )
    attended = join_heads(head_out).astype(jnp.bfloat16)
    branch_attn = lax.psum(
        jnp.einsum("ish,hd->isd", attended, out_full, preferred_element_type=jnp.float32), "tensor"
    )
    middle = tokens + gains[2] * branch_attn
    normed2, inv_std2, pre_norm2 = norm_fwd(middle, gains[1])
    normed2_low = pre_norm2.astype(jnp.bfloat16)
    pre_act = jnp.einsum("isd,df->isf", normed2_low, up_full, preferred_element_type=jnp.float32)
    act_val, act_slope = gelu_parts(pre_act)
    act_low = act_val.astype(jnp.bfloat16)
    branch_mlp = lax.psum(
        jnp.einsum("isf,fd->isd", act_low, down_full, preferred_element_type=jnp.float32), "tensor"
    )
    output = middle + gains[3] * branch_mlp
    qkv_full, out_full, up_full, down_full = (
        lax.all_gather(w_qkv, "fsdp", axis=0, tiled=True),
        lax.all_gather(w_out, "fsdp", axis=1, tiled=True),
        lax.all_gather(w_up, "fsdp", axis=0, tiled=True),
        lax.all_gather(w_down, "fsdp", axis=1, tiled=True),
    )
    grad_mlp = (gains[3] * cotangent).astype(jnp.bfloat16)
    grad_hidden = jnp.einsum("isd,fd->isf", grad_mlp, down_full, preferred_element_type=jnp.float32)
    grad_pre = (grad_hidden * act_slope).astype(jnp.bfloat16)
    grad_n2 = lax.psum(
        jnp.einsum("isf,df->isd", grad_pre, up_full, preferred_element_type=jnp.float32), "tensor"
    )
    middle_part, grad_gain2 = norm_back(grad_n2, gains[1], normed2, inv_std2)
    grad_middle = cotangent + middle_part
    grad_branch = (gains[2] * grad_middle).astype(jnp.bfloat16)
    grad_att = jnp.einsum(
        "isd,hd->ish", grad_branch, out_full, preferred_element_type=jnp.float32
    ).astype(jnp.bfloat16)
    keys_vals, key_live = (
        lax.all_gather(kv_local, "context", axis=1, tiled=True),
        lax.all_gather(key_flag, "context", axis=1, tiled=True),
    )
    grad_heads_all = split_heads(grad_att)
    key_heads = split_heads(keys_vals[:, :, 0])
    value_heads = split_heads(keys_vals[:, :, 1])

    def head_backward(operands):
        queries, key_rows, value_rows, head_total, grad_heads = operands
        scores = (
            jnp.einsum("iqd,ikd->iqk", queries, key_rows, preferred_element_type=jnp.float32)
            * score_scale
        )
        scores = jnp.where(key_live[:, None, :] > 0, scores, -1e30)
        prob_full = jnp.exp(scores - head_total)
        grad_prob = jnp.einsum(
            "iqd,ikd->iqk", grad_heads, value_rows, preferred_element_type=jnp.float32
        )
        row_delta = jnp.sum(prob_full * grad_prob, axis=-1, keepdims=True)
        grad_score = (prob_full * (grad_prob - row_delta)).astype(jnp.bfloat16)
        grad_query = (
            jnp.einsum("iqk,ikd->iqd", grad_score, key_rows, preferred_element_type=jnp.float32)
            * score_scale
        )
        grad_key = (
            jnp.einsum("iqk,iqd->ikd", grad_score, queries, preferred_element_type=jnp.float32)
            * score_scale
        )
        grad_value = jnp.einsum(
            "iqk,iqd->ikd",
            prob_full.astype(jnp.bfloat16),
            grad_heads,
            preferred_element_type=jnp.float32,
        )
        return (grad_query, grad_key, grad_value)

    grad_query, grad_key, grad_value = lax.map(
        head_backward, (query_heads, key_heads, value_heads, log_total, grad_heads_all)
    )
    key_terms = jnp.stack([join_heads(grad_key), join_heads(grad_value)], axis=2)
    key_grads = lax.psum_scatter(key_terms, "context", scatter_dimension=1, tiled=True)
    grad_qkv = jnp.concatenate([join_heads(grad_query)[:, :, None], key_grads], axis=2).astype(
        jnp.bfloat16
    )
    grad_n1 = lax.psum(
        jnp.einsum("isjh,djh->isd", grad_qkv, qkv_full, preferred_element_type=jnp.float32),
        "tensor",
    )
    input_part, grad_gain1 = norm_back(grad_n1, gains[0], normed1, inv_std1)
    grad_tokens = grad_middle + input_part
    grad_gain3 = jnp.sum(grad_middle * branch_attn, axis=(0, 1))
    grad_gain4 = jnp.sum(cotangent * branch_mlp, axis=(0, 1))
    gain_terms = jnp.stack([grad_gain1, grad_gain2, grad_gain3, grad_gain4], axis=0)
    term_qkv = jnp.einsum(
        "tjh,td->jhd",
        grad_qkv.reshape(tok_rows, 3, half_width),
        normed1_low.reshape(tok_rows, D),
        preferred_element_type=jnp.float32,
    )
    term_out = jnp.einsum(
        "th,td->hd",
        attended.reshape(tok_rows, half_width),
        grad_branch.reshape(tok_rows, D),
        preferred_element_type=jnp.float32,
    )[None]
    term_up = jnp.einsum(
        "tjh,td->jhd",
        grad_pre.reshape(tok_rows, up_blocks, half_width),
        normed2_low.reshape(tok_rows, D),
        preferred_element_type=jnp.float32,
    )
    term_down = jnp.einsum(
        "tjh,td->jhd",
        act_low.reshape(tok_rows, up_blocks, half_width),
        grad_mlp.reshape(tok_rows, D),
        preferred_element_type=jnp.float32,
    )
    block_terms = jnp.concatenate([term_qkv, term_out, term_up, term_down], axis=0)
    fsdp_count = lax.axis_size("fsdp")
    context_count = lax.axis_size("context")
    slot_count = NBLK // context_count
    row_count = half_width // fsdp_count
    onehot = (owner[:, None] == jnp.arange(NBLK, dtype=jnp.int32)[None, :]).astype(jnp.int32)
    block_of = jnp.sum(onehot * jnp.arange(NBLK, dtype=jnp.int32)[:, None], axis=0)
    shaped_terms = block_terms.reshape(NBLK, fsdp_count, row_count, D)
    placed = shaped_terms[
        block_of.reshape(context_count, slot_count)[None, :, :],
        jnp.arange(fsdp_count)[:, None, None],
    ]
    placed = placed.reshape(-1, D)
    summed, gain_grad = (
        lax.psum_scatter(placed, ("fsdp", "context"), scatter_dimension=0, tiled=True),
        lax.psum_scatter(gain_terms, ("fsdp", "context"), scatter_dimension=1, tiled=True),
    )
    grad_mine = summed.reshape(slot_count, row_count, D)
    grad_half = lax.all_gather(grad_mine, "fsdp", axis=1, tiled=True)
    grad_full = lax.all_gather(grad_half[:, None], "tensor", axis=1, tiled=True).reshape(
        slot_count, D, D
    )
    row_offset = lax.axis_index("tensor") * half_width + lax.axis_index("fsdp") * row_count
    tokens_all = images * fsdp_count * SEQ
    highest = lax.Precision.HIGHEST
    left_new = 0.5 * stat_left[:, 0] + 0.5 / tokens_all * jnp.einsum(
        "sra,sba->srb", grad_mine, grad_full, precision=highest
    )
    grad_cols = lax.dynamic_slice_in_dim(grad_full, row_offset, row_count, 2)
    right_new = 0.5 * stat_right[:, 0] + 0.5 / tokens_all * jnp.einsum(
        "sar,sab->srb", grad_cols, grad_full, precision=highest
    )
    inner_prod = jnp.einsum("sra,sab->srb", root_left[:, 0], grad_full, precision=highest)
    update = jnp.einsum("srb,sbc->src", inner_prod, root_right, precision=highest)
    square_sum = lax.psum(jnp.sum(update * update, axis=(1, 2)), ("fsdp", "tensor"))
    factor = 1.0 * lax.rsqrt(square_sum / (D * D) + 1e-06)
    weight_new = master[:, 0] - factor[:, None, None] * update
    share_width = gain_grad.shape[1]
    gain_index = lax.axis_index(("fsdp", "context"))
    gain_mine = lax.dynamic_slice_in_dim(gains, gain_index * share_width, share_width, 1)
    state_new = 0.5 * gain_state + 0.5 * gain_grad * gain_grad / tokens_all
    gain_new = gain_mine - 0.1 * gain_grad * lax.rsqrt(tokens_all * state_new)
    return (
        output,
        grad_tokens,
        grad_mine[:, None],
        left_new[:, None],
        right_new[:, None],
        weight_new[:, None],
        gain_grad,
        state_new,
        gain_new,
    )


def solution(mesh):
    return jax.shard_map(
        per_device,
        mesh=mesh,
        in_specs=(
            P("fsdp", "context", None),
            P("fsdp", "context", None),
            P(),
            P("fsdp", None, "tensor"),
            P("tensor", "fsdp"),
            P("fsdp", "tensor"),
            P("tensor", "fsdp"),
            P("fsdp", "context"),
            P(),
            P("context", "tensor", "fsdp", None),
            P("context", "tensor", "fsdp", None),
            P("context", "tensor", "fsdp", None),
            P("context", None, None),
            P("context", "tensor", "fsdp", None),
            P(None, ("fsdp", "context")),
        ),
        out_specs=(
            P("fsdp", "context", None),
            P("fsdp", "context", None),
            P("context", "tensor", "fsdp", None),
            P("context", "tensor", "fsdp", None),
            P("context", "tensor", "fsdp", None),
            P("context", "tensor", "fsdp", None),
            P(None, ("fsdp", "context")),
            P(None, ("fsdp", "context")),
            P(None, ("fsdp", "context")),
        ),
        check_vma=False,
    )
```

profile of v0, /device:TPU:0, one launch (start us, length us, event | category | flops | bytes accessed | tf_op | source)
XLA Modules:
  0.0 1557.0 jit_solution(10948431820645879818)
XLA Ops:
  13.4 62.4 %all-gather.10.cloned.1.call-done = bf16[1024,3,512]{2,0,1:T(8,128)(2,1)} async-done(((bf16[256,3,512]{2,0,1:T(8,128)(2,1)}), bf16[1024,3,512]{2,0,1:T(8,128)(2,1)}) %all-gather.10.cloned.1.call-update) | async-done | bytes 3145744 | tf_op jit(solution)/shard_map/all_gather | solution.py:67
  97.7 76.8 %all-gather.12.cloned.1.call-done = bf16[3,1408,2,512]{3,1,2,0:T(8,128)(2,1)} async-done(((bf16[3,352,2,512]{3,1,2,0:T(8,128)(2,1)}), bf16[3,1408,2,512]{3,1,2,0:T(8,128)(2,1)}) %all-gather.12.cloned.1.call-update) | async-done | bytes 8650768 | tf_op jit(solution)/shard_map/all_gather | solution.py:83
  204.1 55.4 %while.26 = (s32[]{:T(128)}, bf16[8,3,352,64]{2,3,1,0:T(8,128)(2,1)}, f32[8,3,352,1]{2,1,3,0:T(4,128)S(1)}, bf16[3,1408]{1,0:T(4,128)(2,1)S(1)}, bf16[8,3,352,64...) while((s32[]{:T(128)}, ...), condition=%wide.region_5.6_spmd, body=%wide.region_2.5_spmd.sunk | while | flops 398478432 | bytes 19434328 | solution.py:102
  272.7 22.9 %all-reduce.5.cloned.1.call-done = f32[3,352,1024]{2,1,0:T(8,128)} async-done(((f32[3,352,1024]{2,1,0:T(8,128)}), f32[3,352,1024]{2,1,0:T(8,128)}) %all-reduce.5.cloned.1.call-update) | async-done | bytes 4325392 | tf_op jit(solution)/shard_map/psum | solution.py:107
  303.7 75.3 %all-gather.16.cloned.1.call-done = bf16[1024,2048]{1,0:T(8,128)(2,1)} async-done(((bf16[256,2048]{1,0:T(8,128)(2,1)}), bf16[1024,2048]{1,0:T(8,128)(2,1)}) %all-gather.16.cloned.1.call-update) | async-done | bytes 4194320 | tf_op jit(solution)/shard_map/all_gather | solution.py:69
  379.0 10.5 multiply_convert_fusion.1
  389.5 70.2 %all-gather.18.cloned.1.call-done = bf16[2048,1024]{1,0:T(8,128)(2,1)} async-done(((bf16[2048,256]{1,0:T(8,128)(2,1)}), bf16[2048,1024]{1,0:T(8,128)(2,1)}) %all-gather.18.cloned.1.call-update) | async-done | bytes 4194320 | tf_op jit(solution)/shard_map/all_gather | solution.py:70
  459.7 10.6 fusion.53
  478.9 26.7 %all-reduce.7.cloned.1.call-done = f32[3,352,1024]{2,1,0:T(8,128)} async-done(((f32[3,352,1024]{2,1,0:T(8,128)}), f32[3,352,1024]{2,1,0:T(8,128)}) %all-reduce.7.cloned.1.call-update) | async-done | bytes 4325392 | tf_op jit(solution)/shard_map/psum | solution.py:129
  525.8 101.5 %while.27 = (s32[]{:T(128)}, bf16[8,3,352,64]{2,3,1,0:T(8,128)(2,1)}, f32[8,3,1408,64]{2,3,0,1:T(8,128)}, f32[8,3,1408,64]{2,3,0,1:T(8,128)}, bf16[3,1408]{1,0:T...) while((s32[]{:T(128)}, ...), condition=%wide.region_15.16_spmd, body=%wide.region_13.15_spmd.sunk | while | flops 965305472 | bytes 49321456 | solution.py:175
  645.6 12.7 pad_maximum_fusion.1
  679.2 10.5 fusion.57
  708.7 109.0 %reduce-scatter.6.cloned.1.call-done = f32[3,352,2,512]{3,1,2,0:T(8,128)} async-done(((f32[3,1408,2,512]{3,1,2,0:T(8,128)}), f32[3,352,2,512]{3,1,2,0:T(8,128)}) %reduce-scatter.6.cloned.1.call-update) | async-done | bytes 4325392 | tf_op jit(solution)/shard_map/reduce_scatter | solution.py:179
  838.0 19.2 %gather_fusion = f32[48,128,1024]{2,1,0:T(8,128)} fusion(f32[12,4,128,1024]{3,2,1,0:T(8,128)} %pad_maximum_fusion, s32[48]{0:T(128)S(1)} %reshape.174), kind=kCustom, calls=%fused_computation | custom fusion | bytes 50332032 | tf_op jit(solution)/shard_map/gather | solution.py:224
  857.3 10.3 fusion.61
  873.0 346.0 %reduce-scatter.8.cloned.1.call-done = f32[384,1024]{1,0:T(8,128)} async-done(((f32[6144,1024]{1,0:T(8,128)}), f32[384,1024]{1,0:T(8,128)}) %reduce-scatter.8.cloned.1.call-update) | async-done | bytes 1572880 | tf_op jit(solution)/shard_map/reduce_scatter | solution.py:230
  1219.1 41.5 %all-reduce.9.cloned.1.call-done = (f32[3,352,1024]{2,1,0:T(8,128)}, f32[3,352,1024]{2,1,0:T(8,128)}) async-done(((f32[3,352,1024]{2,1,0:T(8,128)}, f32[3,352,1024]{2,1,0:T(8,128)}), (f32[3,352,1024]{2,1,0:T(8,128)}, f32[3,352,1024]{2,1,0:T(8,128)})) %all-reduce.9.cloned.1.call-update) | async-done | bytes 8650768 | tf_op jit(solution)/shard_map/psum | solution.py:116
  1274.1 105.2 %all-gather.20.cloned.1.call-done = f32[3,512,1024]{2,1,0:T(8,128)} async-done(((f32[3,128,1024]{2,1,0:T(8,128)}), f32[3,512,1024]{2,1,0:T(8,128)}) %all-gather.20.cloned.1.call-update) | async-done | bytes 6291472 | tf_op jit(solution)/shard_map/all_gather | solution.py:234
  1386.5 70.3 %reduce-scatter.10.cloned.1.call-done = f32[64,4]{1,0:T(8,128)} async-done(((f32[1024,4]{1,0:T(8,128)}), f32[64,4]{1,0:T(8,128)}) %reduce-scatter.10.cloned.1.call-update) | async-done | bytes 1040
  1459.1 20.7 %all-gather.22.cloned.1.call-done = f32[3,1024,1024]{2,1,0:T(8,128)} async-done(((f32[3,512,1024]{2,1,0:T(8,128)}), f32[3,1024,1024]{2,1,0:T(8,128)}) %all-gather.22.cloned.1.call-update) | async-done | bytes 12582928 | tf_op jit(solution)/shard_map/all_gather | solution.py:235
  1489.8 10.7 multiply_reduce_fusion.11
  1500.5 17.3 %psum.39 = f32[3]{0:T(128)S(1)} all-reduce(f32[3]{0:T(128)S(1)} %get-tuple-element.281), channel_id=1, replica_groups=mesh['fsdp'=4,'context'=4,'tensor'=2] {'fsdp','tensor'}, use_global_device_ids=true, to_apply=%region_23.24 | all-reduce | flops 3 | bytes 24 | tf_op jit(solution)/shard_map/psum | solution.py:250
  1520.9 17.4 %fusion.88 = f32[3,1,128,1024]{3,2,1,0:T(8,128)} fusion(f32[3,1,128,1024]{3,2,1,0:T(8,128)S(1)} %copy-done.14, f32[3,128,1024]{2,1,0:T(8,128)S(1)} %bitcast.291, f32[3,1024,1024]{2,1,0:T(8,128)} %all-gather.22.cloned.1.call-done), kind=kOutput, calls=%fused_computation.123 | convolution fusion | flops 4833017856 | bytes 17301504 | tf_op jit(solution)/shard_map/sra,sba->srb/dot_general | solution.py:241
  1538.3 12.0 fusion.87
  (279 shorter events, 383.9 us)
Async XLA Ops:
  7.2 1472.6 %copy-start = (f32[3,1,128,1024]{3,2,1,0:T(8,128)S(1)}, f32[3,1,128,1024]{3,2,1,0:T(8,128)}, u32[]{:S(2)}) copy-start(f32[3,1,128,1024]{3,2,1,0:T(8,128)} %param.30) | copy-start | bytes 4718596
  7.2 68.6 %all-gather.10.cloned.1.call-start = ((), (), s32[]{:S(2)}) async-start(), calls=%async_computation.3 | async-start | bytes 3932160 | tf_op jit(solution)/shard_map/all_gather | solution.py:67
  7.9 166.6 %all-gather.12.cloned.1.call-start = ((), (), s32[]{:S(2)}) async-start(), calls=%async_computation.4 | async-start | bytes 10813440 | tf_op jit(solution)/shard_map/all_gather | solution.py:83
  10.5 72.1 %copy-start.18 = (f32[3,352]{1,0:T(4,128)}, f32[3,352]{1,0:T(4,128)S(1)}, u32[]{:S(2)}) copy-start(f32[3,352]{1,0:T(4,128)S(1)} %broadcast_multiply_fusion.5) | copy-start | bytes 12676
  13.3 69.3 %copy-start.20 = (f32[3,352]{1,0:T(4,128)}, f32[3,352]{1,0:T(4,128)S(1)}, u32[]{:S(2)}) copy-start(f32[3,352]{1,0:T(4,128)S(1)} %add_rsqrt_fusion.1) | copy-start | bytes 12676
  13.4 69.3 %copy-start.22 = (f32[1,1024]{1,0:T(1,128)}, f32[1,1024]{1,0:T(1,128)S(1)}, u32[]{:S(2)}) copy-start(f32[1,1024]{1,0:T(1,128)S(1)} %get-tuple-element.276) | copy-start | bytes 12292
  13.4 255.1 %copy-start.24 = (f32[1,1024]{1,0:T(1,128)}, f32[1,1024]{1,0:T(1,128)S(1)}, u32[]{:S(2)}) copy-start(f32[1,1024]{1,0:T(1,128)S(1)} %get-tuple-element.275) | copy-start | bytes 12292
  85.9 176.0 %all-gather.14.cloned.1.call-start = ((), (), s32[]{:S(2)}) async-start(), calls=%async_computation.5 | async-start | bytes 1310720 | tf_op jit(solution)/shard_map/all_gather | solution.py:68
  86.6 209.0 %all-reduce.5.cloned.1.call-start = ((), (), s32[]{:S(2)}) async-start(), calls=%async_computation.6 | async-start | bytes 8650752 | tf_op jit(solution)/shard_map/psum | solution.py:107
  266.8 112.2 %all-gather.16.cloned.1.call-start = ((), (), s32[]{:S(2)}) async-start(), calls=%async_computation.7 | async-start | bytes 5242880 | tf_op jit(solution)/shard_map/all_gather | solution.py:69
  267.4 192.2 %all-gather.18.cloned.1.call-start = ((), (), s32[]{:S(2)}) async-start(), calls=%async_computation.8 | async-start | bytes 5242880 | tf_op jit(solution)/shard_map/all_gather | solution.py:70
  268.0 237.6 %all-reduce.7.cloned.1.call-start = ((), (), s32[]{:S(2)}) async-start(), calls=%async_computation.9 | async-start | bytes 8650752 | tf_op jit(solution)/shard_map/psum | solution.py:129
  478.6 339.1 %reduce-scatter.6.cloned.1.call-start = ((), (), s32[]{:S(2)}) async-start(), calls=%async_computation.10 | async-start | bytes 21626880 | tf_op jit(solution)/shard_map/reduce_scatter | solution.py:179
  658.3 560.7 %reduce-scatter.8.cloned.1.call-start = ((), (), s32[]{:S(2)}) async-start(), calls=%async_computation.11 | async-start | bytes 26738688 | tf_op jit(solution)/shard_map/reduce_scatter | solution.py:230
  708.7 111.7 %copy-start.16 = (bf16[3,352,1,512]{3,1,2,0:T(8,128)(2,1)S(1)}, bf16[3,352,1,512]{3,1,2,0:T(8,128)(2,1)}, u32[]{:S(2)}) copy-start(bf16[3,352,1,512]{3,1,2,0:T(8,128)(2,1)} %copy.158) | copy-start | bytes 3244036
  708.7 111.7 %copy-start.19 = (f32[3,352]{1,0:T(4,128)S(1)}, f32[3,352]{1,0:T(4,128)}, u32[]{:S(2)}) copy-start(f32[3,352]{1,0:T(4,128)} %copy-done.18) | copy-start | bytes 12676
  708.7 111.7 %copy-start.21 = (f32[3,352]{1,0:T(4,128)S(1)}, f32[3,352]{1,0:T(4,128)}, u32[]{:S(2)}) copy-start(f32[3,352]{1,0:T(4,128)} %copy-done.20) | copy-start | bytes 12676
  708.7 111.7 %copy-start.23 = (f32[1,1024]{1,0:T(1,128)S(1)}, f32[1,1024]{1,0:T(1,128)}, u32[]{:S(2)}) copy-start(f32[1,1024]{1,0:T(1,128)} %copy-done.22) | copy-start | bytes 12292
  857.2 403.4 %all-reduce.9.cloned.1.call-start = ((), (), s32[]{:S(2)}) async-start(), calls=%async_computation.15 | async-start | bytes 17301504 | tf_op jit(solution)/shard_map/psum | solution.py:116
  872.9 506.4 %all-gather.20.cloned.1.call-start = ((), (), s32[]{:S(2)}) async-start(), calls=%async_computation.12 | async-start | bytes 7864320 | tf_op jit(solution)/shard_map/all_gather | solution.py:234
  1219.0 237.9 %reduce-scatter.10.cloned.1.call-start = ((), (), s32[]{:S(2)}) async-start(), calls=%async_computation.14 | async-start | bytes 557056
  1274.0 205.7 %all-gather.22.cloned.1.call-start = ((), (), s32[]{:S(2)}) async-start(), calls=%async_computation.13 | async-start | bytes 18874368 | tf_op jit(solution)/shard_map/all_gather | solution.py:235
  1379.4 78.3 %copy-start.31 = (f32[4,64]{1,0:T(4,128)S(1)}, f32[4,64]{1,0:T(4,128)}, u32[]{:S(2)}) copy-start(f32[4,64]{1,0:T(4,128)} %param.33) | copy-start | bytes 3076
  1457.7 32.1 %copy-start.29 = (f32[4,64]{1,0:T(4,128)}, f32[4,64]{1,0:T(4,128)S(1)}, u32[]{:S(2)}) copy-start(f32[4,64]{1,0:T(4,128)S(1)} %copy.185) | copy-start | bytes 3076
  (29 other events, 204.0 us)
Sparse Core Ops, SparseCore 0:
  9.6 66.1 all-gather.9
  86.0 88.4 all-gather.11
  176.1 30.1 all-gather.13
  266.9 28.5 all-reduce.4
  297.1 81.9 all-gather.15
  380.5 79.0 all-gather.17
  478.8 26.7 all-reduce.6
  658.4 159.2 reduce-scatter.5
  857.3 361.6 reduce-scatter.7
  1222.1 38.3 all-reduce.8
  1262.8 116.5 all-gather.19
  1382.1 74.7 reduce-scatter.9
  1458.5 21.2 all-gather.21
where the time goes:
time: 1570 us; the launch traced here: 1560 us
  waiting for transfers between devices  1030 us (66%)
  matrix products  280 us (18%)
  local copies, waits for them, and re-layouts  113 us (7%)
  other arithmetic  92.7 us (6%)
  blocking collectives  25.4 us (2%)
    reduce_scatter x1, waiting for transfers between devices, per_device(): lax.psum_scatter(placed, ('fsdp', 'context'), scatter_dimension=0, tiled=...  346 us
    reduce_scatter x1, waiting for transfers between devices, per_device(): lax.psum_scatter(key_terms, 'context', scatter_dimension=1, tiled=True)  109 us
    all_gather x1, waiting for transfers between devices, per_device(): grad_half = lax.all_gather(grad_mine, 'fsdp', axis=1, tiled=True)  105 us
    all_gather x1, waiting for transfers between devices, per_device(): lax.all_gather(kv_local, 'context', axis=1, tiled=True)  76.8 us
    all_gather x1, waiting for transfers between devices, per_device(): lax.all_gather(w_up, 'fsdp', axis=0, tiled=True)  75.3 us
    unnamed x14, waiting for transfers between devices  72.9 us
    all_gather x1, waiting for transfers between devices, per_device(): lax.all_gather(w_down, 'fsdp', axis=1, tiled=True)  70.2 us
    all_gather x1, waiting for transfers between devices, per_device(): lax.all_gather(w_qkv, 'fsdp', axis=0, tiled=True)  62.4 us
  transfers between devices with their start and end apart: 13, of which 12 were waited for; matrix products, arithmetic and copies ran while one was open for 13% of the time, Pallas kernels for 0%

commit v1 on v0

--- a/solution.py
+++ b/solution.py
@@ -231,7 +231,12 @@
         lax.psum_scatter(gain_terms, ("fsdp", "context"), scatter_dimension=1, tiled=True),
     )
     grad_mine = summed.reshape(slot_count, row_count, D)
-    grad_half = lax.all_gather(grad_mine, "fsdp", axis=1, tiled=True)
+    ring = [grad_mine]
+    for hop in range(3):
+        ring.append(lax.ppermute(ring[-1], "fsdp", [(dev, (dev + 1) % 4) for dev in range(4)]))
+    grad_half = jnp.roll(
+        jnp.concatenate(ring[::-1], axis=1), (lax.axis_index("fsdp") + 1) * ring[0].shape[1], axis=1
+    )
     grad_full = lax.all_gather(grad_half[:, None], "tensor", axis=1, tiled=True).reshape(
         slot_count, D, D
     )

time: 1570 us -> 1500 us (0.955)
  waiting for transfers between devices: 1030 us -> 949 us
    all_gather x1 -> x0, waiting for transfers between devices: 105 us -> none  [per_device(): grad_half = lax.all_gather(grad_mine, 'fsdp', axis=1, tiled=True)]
    ppermute x0 -> x3, waiting for transfers between devices: none -> 99.9 us  [per_device(): lax.ppermute(ring[-1], 'fsdp', [(dev, (dev + 1) % 4) for dev in range(4)])]
    psum x1, waiting for transfers between devices: 41.5 us -> 0.01 us  [per_device(): lax.psum(jnp.einsum('isf,fd->isd', act_low, down_full, preferred_element_...]
    unnamed x14 -> x13, waiting for transfers between devices: 72.9 us -> 39.1 us
  transfers between devices with their start and end apart: 13 -> 15, of which waited for: 12 -> 13; matrix products, arithmetic and copies ran while one was open for 13% -> 14% of each run, Pallas kernels for 0% -> 0%
where the time goes in v1:
time: 1500 us; the launch traced here: 1490 us
  waiting for transfers between devices  949 us (63%)
  matrix products  281 us (19%)
  local copies, waits for them, and re-layouts  123 us (8%)
  other arithmetic  93.6 us (6%)
  blocking collectives  25.4 us (2%)
  between operations  15 us (1%)
    reduce_scatter x1, waiting for transfers between devices, per_device(): lax.psum_scatter(placed, ('fsdp', 'context'), scatter_dimension=0, tiled=...  346 us
    reduce_scatter x1, waiting for transfers between devices, per_device(): lax.psum_scatter(key_terms, 'context', scatter_dimension=1, tiled=True)  109 us
    ppermute x3, waiting for transfers between devices, per_device(): lax.ppermute(ring[-1], 'fsdp', [(dev, (dev + 1) % 4) for dev in range(4)])  99.9 us
    all_gather x1, waiting for transfers between devices, per_device(): lax.all_gather(kv_local, 'context', axis=1, tiled=True)  76.8 us
    all_gather x1, waiting for transfers between devices, per_device(): lax.all_gather(w_up, 'fsdp', axis=0, tiled=True)  75.4 us
    all_gather x1, waiting for transfers between devices, per_device(): lax.all_gather(w_down, 'fsdp', axis=1, tiled=True)  70.1 us
    all_gather x1, waiting for transfers between devices, per_device(): lax.all_gather(w_qkv, 'fsdp', axis=0, tiled=True)  62.4 us
    unnamed x13, waiting for transfers between devices  39.1 us
  transfers between devices with their start and end apart: 15, of which 13 were waited for; matrix products, arithmetic and copies ran while one was open for 14% of the time, Pallas kernels for 0%

profile of v1, /device:TPU:0, one launch (start us, length us, event | category | flops | bytes accessed | tf_op | source)
XLA Modules:
  0.0 1489.0 jit_solution(5972552066548803473)
XLA Ops:
  13.4 62.4 %all-gather.9.cloned.1.call-done = bf16[1024,3,512]{2,0,1:T(8,128)(2,1)} async-done(((bf16[256,3,512]{2,0,1:T(8,128)(2,1)}), bf16[1024,3,512]{2,0,1:T(8,128)(2,1)}) %all-gather.9.cloned.1.call-update) | async-done | bytes 3145744 | tf_op jit(solution)/shard_map/all_gather | solution.py:67
  97.7 76.8 %all-gather.11.cloned.1.call-done = bf16[3,1408,2,512]{3,1,2,0:T(8,128)(2,1)} async-done(((bf16[3,352,2,512]{3,1,2,0:T(8,128)(2,1)}), bf16[3,1408,2,512]{3,1,2,0:T(8,128)(2,1)}) %all-gather.11.cloned.1.call-update) | async-done | bytes 8650768 | tf_op jit(solution)/shard_map/all_gather | solution.py:83
  204.1 55.3 %while.26 = (s32[]{:T(128)}, bf16[8,3,352,64]{2,3,1,0:T(8,128)(2,1)}, f32[8,3,352,1]{2,1,3,0:T(4,128)S(1)}, bf16[3,1408]{1,0:T(4,128)(2,1)S(1)}, bf16[8,3,352,64...) while((s32[]{:T(128)}, ...), condition=%wide.region_5.6_spmd, body=%wide.region_2.5_spmd.sunk | while | flops 398478432 | bytes 19434328 | solution.py:102
  272.6 23.0 %all-reduce.5.cloned.1.call-done = f32[3,352,1024]{2,1,0:T(8,128)} async-done(((f32[3,352,1024]{2,1,0:T(8,128)}), f32[3,352,1024]{2,1,0:T(8,128)}) %all-reduce.5.cloned.1.call-update) | async-done | bytes 4325392 | tf_op jit(solution)/shard_map/psum | solution.py:107
  303.6 75.4 %all-gather.15.cloned.1.call-done = bf16[1024,2048]{1,0:T(8,128)(2,1)} async-done(((bf16[256,2048]{1,0:T(8,128)(2,1)}), bf16[1024,2048]{1,0:T(8,128)(2,1)}) %all-gather.15.cloned.1.call-update) | async-done | bytes 4194320 | tf_op jit(solution)/shard_map/all_gather | solution.py:69
  379.1 10.5 multiply_convert_fusion.1
  389.6 70.1 %all-gather.17.cloned.1.call-done = bf16[2048,1024]{1,0:T(8,128)(2,1)} async-done(((bf16[2048,256]{1,0:T(8,128)(2,1)}), bf16[2048,1024]{1,0:T(8,128)(2,1)}) %all-gather.17.cloned.1.call-update) | async-done | bytes 4194320 | tf_op jit(solution)/shard_map/all_gather | solution.py:70
  459.7 10.6 fusion.53
  478.9 26.7 %all-reduce.7.cloned.1.call-done = f32[3,352,1024]{2,1,0:T(8,128)} async-done(((f32[3,352,1024]{2,1,0:T(8,128)}), f32[3,352,1024]{2,1,0:T(8,128)}) %all-reduce.7.cloned.1.call-update) | async-done | bytes 4325392 | tf_op jit(solution)/shard_map/psum | solution.py:129
  525.8 101.6 %while.27 = (s32[]{:T(128)}, bf16[8,3,352,64]{2,3,1,0:T(8,128)(2,1)}, f32[8,3,1408,64]{2,3,0,1:T(8,128)}, f32[8,3,1408,64]{2,3,0,1:T(8,128)}, bf16[3,1408]{1,0:T...) while((s32[]{:T(128)}, ...), condition=%wide.region_15.16_spmd, body=%wide.region_13.15_spmd.sunk | while | flops 965305472 | bytes 49321456 | solution.py:175
  645.7 12.7 pad_maximum_fusion.1
  679.3 10.4 fusion.57
  708.5 109.3 %reduce-scatter.6.cloned.1.call-done = f32[3,352,2,512]{3,1,2,0:T(8,128)} async-done(((f32[3,1408,2,512]{3,1,2,0:T(8,128)}), f32[3,352,2,512]{3,1,2,0:T(8,128)}) %reduce-scatter.6.cloned.1.call-update) | async-done | bytes 4325392 | tf_op jit(solution)/shard_map/reduce_scatter | solution.py:179
  838.1 19.1 %gather_fusion = f32[48,128,1024]{2,1,0:T(8,128)} fusion(f32[12,4,128,1024]{3,2,1,0:T(8,128)} %pad_maximum_fusion, s32[48]{0:T(128)S(1)} %reshape.174), kind=kCustom, calls=%fused_computation | custom fusion | bytes 50332032 | tf_op jit(solution)/shard_map/gather | solution.py:224
  873.4 345.5 %reduce-scatter.8.cloned.1.call-done = f32[384,1024]{1,0:T(8,128)} async-done(((f32[6144,1024]{1,0:T(8,128)}), f32[384,1024]{1,0:T(8,128)}) %reduce-scatter.8.cloned.1.call-update) | async-done | bytes 1572880 | tf_op jit(solution)/shard_map/reduce_scatter | solution.py:230
  1219.0 38.1 %collective-permute-done = f32[3,128,1024]{2,1,0:T(8,128)S(1)} collective-permute-done((f32[3,128,1024]{2,1,0:T(8,128)}, f32[3,128,1024]{2,1,0:T(8,128)S(1)}, u32[]{:S(2)}, u32[]{:S(2)}) %collective-permute-start) | collective-permute-done | bytes 1572896 | tf_op jit(solution)/shard_map/ppermute | solution.py:236
  1258.3 37.2 %collective-permute-done.1 = f32[3,128,1024]{2,1,0:T(8,128)} collective-permute-done((f32[3,128,1024]{2,1,0:T(8,128)S(1)}, f32[3,128,1024]{2,1,0:T(8,128)}, u32[]{:S(2)}, u32[]{:S(2)}) %collective-permute-start.1) | collective-permute-done | bytes 1572896 | tf_op jit(solution)/shard_map/ppermute | solution.py:236
  1309.1 24.5 %collective-permute-done.2 = f32[3,128,1024]{2,1,0:T(8,128)} collective-permute-done((f32[3,128,1024]{2,1,0:T(8,128)}, f32[3,128,1024]{2,1,0:T(8,128)}, u32[]{:S(2)}, u32[]{:S(2)}) %collective-permute-start.2) | collective-permute-done | bytes 1572896 | tf_op jit(solution)/shard_map/ppermute | solution.py:236
  1350.8 36.5 %reduce-scatter.10.cloned.1.call-done = f32[64,4]{1,0:T(8,128)} async-done(((f32[1024,4]{1,0:T(8,128)}), f32[64,4]{1,0:T(8,128)}) %reduce-scatter.10.cloned.1.call-update) | async-done | bytes 1040
  1389.5 20.7 %all-gather.19.cloned.1.call-done = f32[3,1024,1024]{2,1,0:T(8,128)} async-done(((f32[3,512,1024]{2,1,0:T(8,128)}), f32[3,1024,1024]{2,1,0:T(8,128)}) %all-gather.19.cloned.1.call-update) | async-done | bytes 12582928 | tf_op jit(solution)/shard_map/all_gather | solution.py:240
  1420.3 11.4 multiply_reduce_fusion.11
  1431.7 17.3 %psum.39 = f32[3]{0:T(128)S(1)} all-reduce(f32[3]{0:T(128)S(1)} %get-tuple-element.281), channel_id=1, replica_groups=mesh['fsdp'=4,'context'=4,'tensor'=2] {'fsdp','tensor'}, use_global_device_ids=true, to_apply=%region_23.24 | all-reduce | flops 3 | bytes 24 | tf_op jit(solution)/shard_map/psum | solution.py:255
  1452.6 17.4 %fusion.88 = f32[3,1,128,1024]{3,2,1,0:T(8,128)} fusion(f32[3,1,128,1024]{3,2,1,0:T(8,128)S(1)} %copy-done.16, f32[3,128,1024]{2,1,0:T(8,128)S(1)} %bitcast.284, f32[3,1024,1024]{2,1,0:T(8,128)} %all-gather.19.cloned.1.call-done), kind=kOutput, calls=%fused_computation.123 | convolution fusion | flops 4833017856 | bytes 17301504 | tf_op jit(solution)/shard_map/sra,sba->srb/dot_general | solution.py:246
  1470.0 12.0 fusion.87
  (295 shorter events, 406.1 us)
Async XLA Ops:
  7.2 1403.0 %copy-start = (f32[3,1,128,1024]{3,2,1,0:T(8,128)S(1)}, f32[3,1,128,1024]{3,2,1,0:T(8,128)}, u32[]{:S(2)}) copy-start(f32[3,1,128,1024]{3,2,1,0:T(8,128)} %param.30) | copy-start | bytes 4718596
  7.2 68.6 %all-gather.9.cloned.1.call-start = ((), (), s32[]{:S(2)}) async-start(), calls=%async_computation.3 | async-start | bytes 3932160 | tf_op jit(solution)/shard_map/all_gather | solution.py:67
  7.9 166.6 %all-gather.11.cloned.1.call-start = ((), (), s32[]{:S(2)}) async-start(), calls=%async_computation.4 | async-start | bytes 10813440 | tf_op jit(solution)/shard_map/all_gather | solution.py:83
  10.5 72.1 %copy-start.20 = (f32[3,352]{1,0:T(4,128)}, f32[3,352]{1,0:T(4,128)S(1)}, u32[]{:S(2)}) copy-start(f32[3,352]{1,0:T(4,128)S(1)} %broadcast_multiply_fusion.5) | copy-start | bytes 12676
  13.3 69.3 %copy-start.22 = (f32[3,352]{1,0:T(4,128)}, f32[3,352]{1,0:T(4,128)S(1)}, u32[]{:S(2)}) copy-start(f32[3,352]{1,0:T(4,128)S(1)} %add_rsqrt_fusion.1) | copy-start | bytes 12676
  13.4 69.3 %copy-start.24 = (f32[1,1024]{1,0:T(1,128)}, f32[1,1024]{1,0:T(1,128)S(1)}, u32[]{:S(2)}) copy-start(f32[1,1024]{1,0:T(1,128)S(1)} %get-tuple-element.276) | copy-start | bytes 12292
  13.4 255.0 %copy-start.26 = (f32[1,1024]{1,0:T(1,128)}, f32[1,1024]{1,0:T(1,128)S(1)}, u32[]{:S(2)}) copy-start(f32[1,1024]{1,0:T(1,128)S(1)} %get-tuple-element.275) | copy-start | bytes 12292
  85.9 175.9 %all-gather.13.cloned.1.call-start = ((), (), s32[]{:S(2)}) async-start(), calls=%async_computation.5 | async-start | bytes 1310720 | tf_op jit(solution)/shard_map/all_gather | solution.py:68
  86.6 209.0 %all-reduce.5.cloned.1.call-start = ((), (), s32[]{:S(2)}) async-start(), calls=%async_computation.6 | async-start | bytes 8650752 | tf_op jit(solution)/shard_map/psum | solution.py:107
  266.7 112.3 %all-gather.15.cloned.1.call-start = ((), (), s32[]{:S(2)}) async-start(), calls=%async_computation.7 | async-start | bytes 5242880 | tf_op jit(solution)/shard_map/all_gather | solution.py:69
  267.3 192.3 %all-gather.17.cloned.1.call-start = ((), (), s32[]{:S(2)}) async-start(), calls=%async_computation.8 | async-start | bytes 5242880 | tf_op jit(solution)/shard_map/all_gather | solution.py:70
  267.9 237.7 %all-reduce.7.cloned.1.call-start = ((), (), s32[]{:S(2)}) async-start(), calls=%async_computation.9 | async-start | bytes 8650752 | tf_op jit(solution)/shard_map/psum | solution.py:129
  478.6 339.1 %reduce-scatter.6.cloned.1.call-start = ((), (), s32[]{:S(2)}) async-start(), calls=%async_computation.10 | async-start | bytes 21626880 | tf_op jit(solution)/shard_map/reduce_scatter | solution.py:179
  658.4 560.5 %reduce-scatter.8.cloned.1.call-start = ((), (), s32[]{:S(2)}) async-start(), calls=%async_computation.11 | async-start | bytes 26738688 | tf_op jit(solution)/shard_map/reduce_scatter | solution.py:230
  708.5 112.0 %copy-start.18 = (bf16[3,352,1,512]{3,1,2,0:T(8,128)(2,1)S(1)}, bf16[3,352,1,512]{3,1,2,0:T(8,128)(2,1)}, u32[]{:S(2)}) copy-start(bf16[3,352,1,512]{3,1,2,0:T(8,128)(2,1)} %copy.158) | copy-start | bytes 3244036
  708.5 112.0 %copy-start.21 = (f32[3,352]{1,0:T(4,128)S(1)}, f32[3,352]{1,0:T(4,128)}, u32[]{:S(2)}) copy-start(f32[3,352]{1,0:T(4,128)} %copy-done.20) | copy-start | bytes 12676
  708.5 112.0 %copy-start.23 = (f32[3,352]{1,0:T(4,128)S(1)}, f32[3,352]{1,0:T(4,128)}, u32[]{:S(2)}) copy-start(f32[3,352]{1,0:T(4,128)} %copy-done.22) | copy-start | bytes 12676
  708.5 112.0 %copy-start.25 = (f32[1,1024]{1,0:T(1,128)S(1)}, f32[1,1024]{1,0:T(1,128)}, u32[]{:S(2)}) copy-start(f32[1,1024]{1,0:T(1,128)} %copy-done.24) | copy-start | bytes 12292
  857.3 438.2 %all-reduce.9.cloned.1.call-start = ((), (), s32[]{:S(2)}) async-start(), calls=%async_computation.14 | async-start | bytes 17301504 | tf_op jit(solution)/shard_map/psum | solution.py:116
  873.3 514.0 %reduce-scatter.10.cloned.1.call-start = ((), (), s32[]{:S(2)}) async-start(), calls=%async_computation.13 | async-start | bytes 557056
  1218.9 38.2 %collective-permute-start = (f32[3,128,1024]{2,1,0:T(8,128)}, f32[3,128,1024]{2,1,0:T(8,128)S(1)}, u32[]{:S(2)}, u32[]{:S(2)}) collective-permute-start(f32[3,128,1024]{2,1,0:T(8,128)} %bitcast.280), channel_id=1, source_target_pairs={{0,8},{8,16},{16,24},{24,0},{1,9},{9,17},{17,25},{25,1},{2,10},{10... | collective-permute-start | bytes 4718600 | tf_op jit(solution)/shard_map/ppermute | solution.py:236
  1258.2 37.2 %collective-permute-start.1 = (f32[3,128,1024]{2,1,0:T(8,128)S(1)}, f32[3,128,1024]{2,1,0:T(8,128)}, u32[]{:S(2)}, u32[]{:S(2)}) collective-permute-start(f32[3,128,1024]{2,1,0:T(8,128)S(1)} %collective-permute-done), channel_id=1, source_target_pairs={{0,8},{8,16},{16,24},{24,0},{1,9},{9,17},{17,25},{25,1},{2,10},{10... | collective-permute-start | bytes 4718600 | tf_op jit(solution)/shard_map/ppermute | solution.py:236
  1295.5 38.1 %collective-permute-start.2 = (f32[3,128,1024]{2,1,0:T(8,128)}, f32[3,128,1024]{2,1,0:T(8,128)}, u32[]{:S(2)}, u32[]{:S(2)}) collective-permute-start(f32[3,128,1024]{2,1,0:T(8,128)} %collective-permute-done.1), channel_id=1, source_target_pairs={{0,8},{8,16},{16,24},{24,0},{1,9},{9,17},{17,25},{25,1},{2,10},{10... | collective-permute-start | bytes 4718600 | tf_op jit(solution)/shard_map/ppermute | solution.py:236
  1309.0 101.2 %all-gather.19.cloned.1.call-start = ((), (), s32[]{:S(2)}) async-start(), calls=%async_computation.12 | async-start | bytes 18874368 | tf_op jit(solution)/shard_map/all_gather | solution.py:240
  (33 other events, 334.1 us)
Sparse Core Ops, SparseCore 0:
  9.6 66.1 all-gather.8
  86.0 88.4 all-gather.10
  176.1 30.1 all-gather.12
  266.9 28.6 all-reduce.4
  297.1 81.9 all-gather.14
  380.6 79.0 all-gather.16
  478.8 26.7 all-reduce.6
  658.5 159.2 reduce-scatter.5
  857.4 361.4 reduce-scatter.7
  1222.0 38.3 all-reduce.8
  1309.1 78.2 reduce-scatter.9
  1388.8 21.3 all-gather.18
